TPU v7x, 32 devices: a whole 2x2x4 slice. The times are simulated.
32 devices in a mesh: dp: 4 (over x, core), row: 4 (over z), col: 2 (over y).
Axes of the slice: x: 2, y: 2, z: 4, core: 2. Of those that a mesh axis runs over, the one named last changes fastest.
Arguments:
- tokens: bfloat16 [4096, 4096], P(('dp', 'col'), 'row'), may hold values from -6 to 6
- cotangent: bfloat16 [4096, 4096], P(('dp', 'col'), 'row'), may hold values from -6 to 6
- gate_pre: bfloat16 [4096, 14336], P(('dp', 'row'), 'col'), may hold values from -6 to 6
- up_pre: bfloat16 [4096, 14336], P(('dp', 'row'), 'col'), may hold values from -6 to 6
- w_gate: bfloat16 [14336, 4096], P('col', 'row'), may hold values from -0.09375 to 0.09375
- w_up: bfloat16 [14336, 4096], P('col', 'row'), may hold values from -0.09375 to 0.09375
- w_down: bfloat16 [4096, 14336], P('row', 'col'), may hold values from -0.046875 to 0.046875
Outputs:
- d_tokens: bfloat16 [4096, 4096], P(('dp', 'col'), 'row')
- grad_gate: float32 [14336, 4096], P(('col', 'dp'), 'row')
- grad_up: float32 [14336, 4096], P(('col', 'dp'), 'row')
- grad_down: float32 [4096, 14336], P(('row', 'dp'), 'col')
All inputs are finite; a program needn't handle non-finite values.
Results may differ from a plain program's by a relative error of at most 0.02.
Values may be sent and summed in bfloat16 or wider, within the bound.
A program may use at most 256 MiB of HBM per device.

v0:
```python
import jax
import jax.numpy as jnp
from jax import lax
from jax.sharding import PartitionSpec as P


def contract_tokens(left, right):
    return lax.dot_general(
        left, right, (((0,), (0,)), ((), ())), preferred_element_type=jnp.float32
    )


def local_grads(hidden_grad, gate_pre, up_pre):
    gate_value = gate_pre.astype(jnp.float32)
    up_value = up_pre.astype(jnp.float32)
    sigmoid_gate = jax.nn.sigmoid(gate_value)
    hidden = (gate_value * sigmoid_gate * up_value).astype(jnp.bfloat16)
    gate_grad = (
        hidden_grad * up_value * sigmoid_gate * (1.0 + gate_value * (1.0 - sigmoid_gate))
    ).astype(jnp.bfloat16)
    up_grad = (hidden_grad * gate_value * sigmoid_gate).astype(jnp.bfloat16)
    return (hidden, gate_grad, up_grad)


def local(tokens, cotangent, gate_pre, up_pre, w_gate, w_up, w_down):
    tok_cols, cot_cols = (
        lax.all_gather(tokens, "col", axis=0, tiled=True),
        lax.all_gather(cotangent, "col", axis=0, tiled=True),
    )
    partial_grad = jnp.dot(cot_cols, w_down, preferred_element_type=jnp.float32)
    hidden_grad = lax.psum(partial_grad.astype(jnp.bfloat16), "row").astype(jnp.float32)
    gate_all, up_all = (
        lax.all_gather(gate_pre, "row", axis=0, tiled=True),
        lax.all_gather(up_pre, "row", axis=0, tiled=True),
    )
    hidden, gate_grad, up_grad = local_grads(hidden_grad, gate_all, up_all)
    d_tokens = lax.psum_scatter(
        (
            jnp.dot(gate_grad, w_gate, preferred_element_type=jnp.float32)
            + jnp.dot(up_grad, w_up, preferred_element_type=jnp.float32)
        ).astype(jnp.bfloat16),
        "col",
        scatter_dimension=0,
        tiled=True,
    )
    grad_down = lax.psum_scatter(
        contract_tokens(cot_cols, hidden).astype(jnp.bfloat16),
        "dp",
        scatter_dimension=0,
        tiled=True,
    ).astype(jnp.float32)
    feature_count = w_gate.shape[1]
    stacked = lax.psum_scatter(
        jnp.concatenate(
            [contract_tokens(gate_grad, tok_cols), contract_tokens(up_grad, tok_cols)], axis=1
        ).astype(jnp.bfloat16),
        "dp",
        scatter_dimension=0,
        tiled=True,
    ).astype(jnp.float32)
    grad_gate = stacked[:, :feature_count]
    grad_up = stacked[:, feature_count:]
    return (d_tokens, grad_gate, grad_up, grad_down)


def solution(mesh):
    placed = (
        P(("dp", "col"), "row"),
        P(("dp", "col"), "row"),
        P(("dp", "row"), "col"),
        P(("dp", "row"), "col"),
        P("col", "row"),
        P("col", "row"),
        P("row", "col"),
    )
    return jax.shard_map(
        local,
        mesh=mesh,
        in_specs=placed,
        out_specs=(
            P(("dp", "col"), "row"),
            P(("col", "dp"), "row"),
            P(("col", "dp"), "row"),
            P(("row", "dp"), "col"),
        ),
        check_vma=False,
    )
```

profile of v0, /device:TPU:0, one launch (start us, length us, event | category | flops | bytes accessed | tf_op | source)
XLA Modules:
  0.0 1437.2 jit_solution(5142862341557165757)
XLA Ops:
  7.2 0.0 all-gather.5.cloned.1.call-start
  7.2 0.7 all-gather.5.cloned.1.call-update
  7.9 0.0 all-gather.9.cloned.1.call-start
  7.9 0.7 all-gather.9.cloned.1.call-update
  8.6 0.0 all-gather.7.cloned.1.call-start
  8.7 0.7 all-gather.7.cloned.1.call-update
  9.4 0.0 all-reduce.2.cloned.1.call-start
  9.4 35.9 %all-gather.5.cloned.1.call-done = bf16[1024,1024]{1,0:T(8,128)(2,1)} async-done(((bf16[512,1024]{1,0:T(8,128)(2,1)}), bf16[1024,1024]{1,0:T(8,128)(2,1)}) %all-gather.5.cloned.1.call-update) | async-done | bytes 2097168 | tf_op jit(solution)/shard_map/all_gather | solution.py:28
  45.4 22.2 %convolution_convert_fusion.2 = bf16[1024,7168]{1,0:T(8,128)(2,1)} fusion(bf16[1024,1024]{1,0:T(8,128)(2,1)} %all-gather.5.cloned.1.call-done, bf16[1024,7168]{1,0:T(8,128)(2,1)} %param.13), kind=kOutput, calls=%fused_computation.21 | convolution fusion | flops 15039725568 | bytes 31457280 | tf_op jit(solution)/shard_map/dot_general | solution.py:30
  67.6 0.0 copy-start
  67.6 0.0 all-reduce.2.cloned.1.call-update
  67.6 0.0 all-gather.11.cloned.1.call-start
  67.7 0.5 all-gather.11.cloned.1.call-update
  68.2 0.0 reduce-scatter.8.cloned.1.call-start
  68.2 231.2 %all-gather.9.cloned.1.call-done = bf16[1024,7168]{1,0:T(8,128)(2,1)} async-done(((bf16[256,7168]{1,0:T(8,128)(2,1)}), bf16[1024,7168]{1,0:T(8,128)(2,1)}) %all-gather.9.cloned.1.call-update) | async-done | bytes 14680080 | tf_op jit(solution)/shard_map/all_gather | solution.py:33
  299.4 252.3 %all-gather.7.cloned.1.call-done = bf16[1024,7168]{1,0:T(8,128)(2,1)} async-done(((bf16[256,7168]{1,0:T(8,128)(2,1)}), bf16[1024,7168]{1,0:T(8,128)(2,1)}) %all-gather.7.cloned.1.call-update) | async-done | bytes 14680080 | tf_op jit(solution)/shard_map/all_gather | solution.py:34
  551.7 0.0 copy-done
  551.7 26.8 %convert_bitcast_fusion = bf16[1024,7168]{0,1:T(8,128)(2,1)} fusion(bf16[1024,1024]{1,0:T(8,128)(2,1)S(1)} %copy-done, bf16[1024,7168]{1,0:T(8,128)(2,1)} %all-gather.7.cloned.1.call-done, bf16[1024,7168]{1,0:T(8,128)(2,1)} %all-gather.9.cloned.1.call-done), kind=kOutput, calls=%fused_computation.17 | convolution fusion | flops 15098445824 | bytes 46137344 | tf_op jit(solution)/shard_map/dot_general | solution.py:8
  578.5 0.0 reduce-scatter.8.cloned.1.call-update
  578.5 0.2 reduce-scatter.6.cloned.1.call-start
  578.7 467.3 %all-reduce.2.cloned.1.call-done = bf16[1024,7168]{1,0:T(8,128)(2,1)} async-done(((bf16[1024,7168]{1,0:T(8,128)(2,1)}), bf16[1024,7168]{1,0:T(8,128)(2,1)}) %all-reduce.2.cloned.1.call-update) | async-done | bytes 14680080 | tf_op jit(solution)/shard_map/psum | solution.py:31
  1046.0 31.7 %fusion.9 = (bf16[1024,7168]{1,0:T(8,128)(2,1)}, bf16[1024,7168]{1,0:T(8,128)(2,1)}) fusion(bf16[1024,7168]{1,0:T(8,128)(2,1)} %all-gather.9.cloned.1.call-done, bf16[1024,7168]{1,0:T(8,128)(2,1)} %all-reduce.2.cloned.1.call-done, bf16[1024,7168]{1,0:T(8,128)(2,1)} %all-gather.7.cloned.1.call-done), kind=kLoop, calls=%fused_computation.15 | loop fusion | flops 117440512 | bytes 73400320 | tf_op jit(solution)/shard_map/convert_element_type | solution.py:21
  1077.7 1.6 all-gather.11.cloned.1.call-done
  1079.4 0.0 copy-start.1
  1079.4 24.4 %convolution_convert_fusion = bf16[7168,1024]{0,1:T(8,128)(2,1)} fusion(bf16[1024,7168]{1,0:T(8,128)(2,1)} %get-tuple-element.8, bf16[1024,1024]{1,0:T(8,128)(2,1)} %all-gather.11.cloned.1.call-done), kind=kOutput, calls=%fused_computation.19 | convolution fusion | flops 15039725568 | bytes 31457280 | tf_op jit(solution)/shard_map/dot_general | solution.py:8
  1103.8 0.0 copy-done.1
  1103.8 23.4 %convolution_convert_fusion.1 = bf16[7168,1024]{0,1:T(8,128)(2,1)} fusion(bf16[1024,7168]{1,0:T(8,128)(2,1)} %get-tuple-element.9, bf16[1024,1024]{1,0:T(8,128)(2,1)S(1)} %copy-done.1), kind=kOutput, calls=%fused_computation.20 | convolution fusion | flops 15039725568 | bytes 31457280 | tf_op jit(solution)/shard_map/dot_general | solution.py:8
  1127.2 21.4 %pad_maximum_fusion = bf16[7168,2048]{0,1:T(8,128)(2,1)} fusion(bf16[7168,1024]{0,1:T(8,128)(2,1)} %convolution_convert_fusion, bf16[7168,1024]{0,1:T(8,128)(2,1)} %convolution_convert_fusion.1), kind=kLoop, calls=%fused_computation.16 | loop fusion | flops 58720256 | bytes 58720256 | tf_op jit(solution)/shard_map/concatenate | solution.py:54
  1148.6 0.0 reduce-scatter.6.cloned.1.call-update
  1148.7 0.0 reduce-scatter.4.cloned.1.call-start
  1148.7 19.2 %fusion.16 = f32[1024,1024]{1,0:T(8,128)S(1)} fusion(bf16[1024,7168]{1,0:T(8,128)(2,1)} %get-tuple-element.9, bf16[7168,1024]{1,0:T(8,128)(2,1)} %param.11), kind=kOutput, calls=%fused_computation.25 | convolution fusion | flops 15032385536 | bytes 33554432 | tf_op jit(solution)/shard_map/dot_general | solution.py:39
  1167.9 21.0 %add_convert_fusion = bf16[1024,1024]{1,0:T(8,128)(2,1)} fusion(f32[1024,1024]{1,0:T(8,128)S(1)} %fusion.16, bf16[1024,7168]{1,0:T(8,128)(2,1)} %get-tuple-element.8, bf16[7168,1024]{1,0:T(8,128)(2,1)} %param.12), kind=kOutput, calls=%fused_computation.22 | convolution fusion | flops 15034482688 | bytes 35651584 | tf_op jit(solution)/shard_map/dot_general | solution.py:40
  1189.0 0.0 reduce-scatter.4.cloned.1.call-update
  1189.0 2.9 reduce-scatter.8.cloned.1.call-done
  1191.9 6.1 copy.13
  1198.1 197.5 %reduce-scatter.6.cloned.1.call-done = bf16[1792,2048]{0,1:T(8,128)(2,1)} async-done(((bf16[7168,2048]{0,1:T(8,128)(2,1)}), bf16[1792,2048]{0,1:T(8,128)(2,1)}) %reduce-scatter.6.cloned.1.call-update) | async-done | bytes 7340048 | tf_op jit(solution)/shard_map/reduce_scatter | solution.py:53
  1395.6 9.7 fusion.15
  1405.2 8.4 copy.12
  1413.6 8.4 copy.11
  1422.0 8.3 reduce-scatter.4.cloned.1.call-done
Async XLA Ops:
  7.2 38.2 %all-gather.5.cloned.1.call-start = ((), (), s32[]{:S(2)}) async-start(), calls=%async_computation.3 | async-start | bytes 3145728 | tf_op jit(solution)/shard_map/all_gather | solution.py:28
  7.9 291.5 %all-gather.9.cloned.1.call-start = ((), (), s32[]{:S(2)}) async-start(), calls=%async_computation.6 | async-start | bytes 18350080 | tf_op jit(solution)/shard_map/all_gather | solution.py:33
  8.6 543.0 %all-gather.7.cloned.1.call-start = ((), (), s32[]{:S(2)}) async-start(), calls=%async_computation.5 | async-start | bytes 18350080 | tf_op jit(solution)/shard_map/all_gather | solution.py:34
  9.4 1036.6 %all-reduce.2.cloned.1.call-start = ((), (), s32[]{:S(2)}) async-start(), calls=%async_computation.4 | async-start | bytes 29360128 | tf_op jit(solution)/shard_map/psum | solution.py:31
  67.6 484.1 %copy-start = (bf16[1024,1024]{1,0:T(8,128)(2,1)S(1)}, bf16[1024,1024]{1,0:T(8,128)(2,1)}, u32[]{:S(2)}) copy-start(bf16[1024,1024]{1,0:T(8,128)(2,1)} %all-gather.5.cloned.1.call-done) | copy-start | bytes 6291460
  67.6 1011.8 %all-gather.11.cloned.1.call-start = ((), (), s32[]{:S(2)}) async-start(), calls=%async_computation.8 | async-start | bytes 3145728 | tf_op jit(solution)/shard_map/all_gather | solution.py:27
  68.2 1123.7 %reduce-scatter.8.cloned.1.call-start = ((), (), s32[]{:S(2)}) async-start(), calls=%async_computation.10 | async-start | bytes 18350080 | tf_op jit(solution)/shard_map/reduce_scatter | solution.py:46
  578.5 817.1 %reduce-scatter.6.cloned.1.call-start = ((), (), s32[]{:S(2)}) async-start(), calls=%async_computation.9 | async-start | bytes 36700160 | tf_op jit(solution)/shard_map/reduce_scatter | solution.py:53
  1079.4 24.4 %copy-start.1 = (bf16[1024,1024]{1,0:T(8,128)(2,1)S(1)}, bf16[1024,1024]{1,0:T(8,128)(2,1)}, u32[]{:S(2)}) copy-start(bf16[1024,1024]{1,0:T(8,128)(2,1)} %all-gather.11.cloned.1.call-done) | copy-start | bytes 6291460
  1148.7 281.7 %reduce-scatter.4.cloned.1.call-start = ((), (), s32[]{:S(2)}) async-start(), calls=%async_computation.7 | async-start | bytes 3145728 | tf_op jit(solution)/shard_map/reduce_scatter | solution.py:37
Sparse Core Ops, SparseCore 0:
  9.5 35.8 all-gather.4
  46.9 252.4 all-gather.8
  301.0 250.6 all-gather.6
  554.0 491.9 all-reduce.1
  1047.4 31.9 all-gather.10
  1081.8 110.0 reduce-scatter.7
  1194.5 201.0 reduce-scatter.5
  1398.4 31.8 reduce-scatter.3
where the time goes:
time: 1440 us
  waiting for transfers between devices  1200 us (83%)
  matrix products  137 us (10%)
  other arithmetic  53.2 us (4%)
  local copies, waits for them, and re-layouts  32.6 us (2%)
    psum x1, waiting for transfers between devices, local(): lax.psum(partial_grad.astype(jnp.bfloat16), 'row').astype(jnp.float32)  467 us
    all_gather x1, waiting for transfers between devices, local(): lax.all_gather(up_pre, 'row', axis=0, tiled=True)  252 us
    all_gather x1, waiting for transfers between devices, local(): lax.all_gather(gate_pre, 'row', axis=0, tiled=True)  231 us
    reduce_scatter x1, waiting for transfers between devices, local(): lax.psum_scatter(jnp.concatenate([contract_tokens(gate_grad, tok_cols), c...  198 us
    dot_general x3, matrix products, contract_tokens(): lax.dot_general(left, right, (((0,), (0,)), ((), ())), preferred_element_...  74.6 us
    all_gather x1, waiting for transfers between devices, local(): lax.all_gather(cotangent, 'col', axis=0, tiled=True)  35.9 us
    convert_element_type x1, other arithmetic, local_grads(): up_grad = (hidden_grad * gate_value * sigmoid_gate).astype(jnp.bfloat16)  31.7 us
  transfers between devices with their start and end apart: 8, of which 8 were waited for; matrix products, arithmetic and copies ran while one was open for 16% of the time, Pallas kernels for 0%

commit v1 on v0

--- a/solution.py
+++ b/solution.py
@@ -28,7 +28,9 @@
         lax.all_gather(cotangent, "col", axis=0, tiled=True),
     )
     partial_grad = jnp.dot(cot_cols, w_down, preferred_element_type=jnp.float32)
-    hidden_grad = lax.psum(partial_grad.astype(jnp.bfloat16), "row").astype(jnp.float32)
+    hidden_grad = jnp.sum(lax.all_gather(partial_grad.astype(jnp.bfloat16), "row"), axis=0).astype(
+        jnp.float32
+    )
     gate_all, up_all = (
         lax.all_gather(gate_pre, "row", axis=0, tiled=True),
         lax.all_gather(up_pre, "row", axis=0, tiled=True),

time: 1440 us -> 1920 us (1.33)
  waiting for transfers between devices: 1200 us -> 1630 us
  other arithmetic: 53.2 us -> 81.7 us
    all_gather x0 -> x1, waiting for transfers between devices: none -> 932 us  [local(): lax.all_gather(partial_grad.astype(jnp.bfloat16), 'row')]
    psum x1 -> x0, waiting for transfers between devices: 467 us -> none  [local(): lax.psum(partial_grad.astype(jnp.bfloat16), 'row').astype(jnp.float32)]
    reduce_scatter x1, waiting for transfers between devices: 198 us -> 167 us  [local(): lax.psum_scatter(jnp.concatenate([contract_tokens(gate_grad, tok_cols), c...]
    reduce_sum x0 -> x1, other arithmetic: none -> 28.2 us  [local(): jnp.sum(lax.all_gather(partial_grad.astype(jnp.bfloat16), 'row'), axis=0)]
  transfers between devices with their start and end apart: 8 -> 8, of which waited for: 8 -> 6; matrix products, arithmetic and copies ran while one was open for 16% -> 14% of each run, Pallas kernels for 0% -> 0%
where the time goes in v1:
time: 1920 us
  waiting for transfers between devices  1630 us (85%)
  matrix products  145 us (8%)
  other arithmetic  81.7 us (4%)
  local copies, waits for them, and re-layouts  33.2 us (2%)
    all_gather x1, waiting for transfers between devices, local(): lax.all_gather(partial_grad.astype(jnp.bfloat16), 'row')  932 us
    all_gather x1, waiting for transfers between devices, local(): lax.all_gather(up_pre, 'row', axis=0, tiled=True)  252 us
    all_gather x1, waiting for transfers between devices, local(): lax.all_gather(gate_pre, 'row', axis=0, tiled=True)  231 us
    reduce_scatter x1, waiting for transfers between devices, local(): lax.psum_scatter(jnp.concatenate([contract_tokens(gate_grad, tok_cols), c...  167 us
    dot_general x3, matrix products, contract_tokens(): lax.dot_general(left, right, (((0,), (0,)), ((), ())), preferred_element_...  78.5 us
  transfers between devices with their start and end apart: 8, of which 6 were waited for; matrix products, arithmetic and copies ran while one was open for 14% of the time, Pallas kernels for 0%

profile of v1, /device:TPU:0, one launch (start us, length us, event | category | flops | bytes accessed | tf_op | source)
XLA Modules:
  0.0 1916.6 jit_solution(2259307189308910332)
XLA Ops:
  7.2 0.0 all-gather.7.cloned.1.call-start
  7.2 0.7 all-gather.7.cloned.1.call-update
  7.9 0.0 all-gather.11.cloned.1.call-start
  7.9 0.7 all-gather.11.cloned.1.call-update
  8.6 0.0 all-gather.9.cloned.1.call-start
  8.7 0.7 all-gather.9.cloned.1.call-update
  9.4 0.0 all-gather.15.cloned.1.call-start
  9.4 35.9 %all-gather.7.cloned.1.call-done = bf16[1024,1024]{1,0:T(8,128)(2,1)} async-done(((bf16[512,1024]{1,0:T(8,128)(2,1)}), bf16[1024,1024]{1,0:T(8,128)(2,1)}) %all-gather.7.cloned.1.call-update) | async-done | bytes 2097168 | tf_op jit(solution)/shard_map/all_gather | solution.py:28
  45.4 22.3 %convolution_convert_fusion.2 = bf16[1024,7168]{1,0:T(8,128)(2,1)} fusion(bf16[1024,1024]{1,0:T(8,128)(2,1)} %all-gather.7.cloned.1.call-done, bf16[1024,7168]{1,0:T(8,128)(2,1)} %param.13), kind=kOutput, calls=%fused_computation.21 | convolution fusion | flops 15039725568 | bytes 31457280 | tf_op jit(solution)/shard_map/dot_general | solution.py:30
  67.6 0.0 copy-start
  67.6 0.0 all-gather.15.cloned.1.call-update
  67.7 0.0 all-gather.13.cloned.1.call-start
  67.7 0.5 all-gather.13.cloned.1.call-update
  68.3 0.0 reduce-scatter.8.cloned.1.call-start
  68.3 231.1 %all-gather.11.cloned.1.call-done = bf16[1024,7168]{1,0:T(8,128)(2,1)} async-done(((bf16[256,7168]{1,0:T(8,128)(2,1)}), bf16[1024,7168]{1,0:T(8,128)(2,1)}) %all-gather.11.cloned.1.call-update) | async-done | bytes 14680080 | tf_op jit(solution)/shard_map/all_gather | solution.py:35
  299.4 252.3 %all-gather.9.cloned.1.call-done = bf16[1024,7168]{1,0:T(8,128)(2,1)} async-done(((bf16[256,7168]{1,0:T(8,128)(2,1)}), bf16[1024,7168]{1,0:T(8,128)(2,1)}) %all-gather.9.cloned.1.call-update) | async-done | bytes 14680080 | tf_op jit(solution)/shard_map/all_gather | solution.py:36
  551.7 0.0 copy-done
  551.7 29.4 %convert_bitcast_fusion = bf16[1024,7168]{0,1:T(8,128)(2,1)} fusion(bf16[1024,1024]{1,0:T(8,128)(2,1)S(1)} %copy-done, bf16[1024,7168]{1,0:T(8,128)(2,1)} %all-gather.9.cloned.1.call-done, bf16[1024,7168]{1,0:T(8,128)(2,1)} %all-gather.11.cloned.1.call-done), kind=kOutput, calls=%fused_computation.17 | convolution fusion | flops 15098445824 | bytes 46137344 | tf_op jit(solution)/shard_map/dot_general | solution.py:8
  581.1 0.0 reduce-scatter.8.cloned.1.call-update
  581.1 12.7 reduce-scatter.6.cloned.1.call-start
  593.8 932.0 %all-gather.15.cloned.1.call-done = bf16[4096,7168]{1,0:T(8,128)(2,1)} async-done(((bf16[1024,7168]{1,0:T(8,128)(2,1)}), bf16[4096,7168]{1,0:T(8,128)(2,1)}) %all-gather.15.cloned.1.call-update) | async-done | bytes 58720272 | tf_op jit(solution)/shard_map/all_gather | solution.py:31
  1525.7 28.2 %reduce_sum.12 = bf16[1024,7168]{1,0:T(8,128)(2,1)} reduce(bf16[4,1024,7168]{2,1,0:T(8,128)(2,1)} %bitcast.14, bf16[]{:T(256)} %constant.1.clone.1), dimensions={0}, to_apply=%region_0.0 | reduce | flops 22020096 | bytes 73400320 | tf_op jit(solution)/shard_map/reduce_sum | solution.py:31
  1553.9 32.9 %fusion.9 = (bf16[1024,7168]{1,0:T(8,128)(2,1)}, bf16[1024,7168]{1,0:T(8,128)(2,1)}) fusion(bf16[1024,7168]{1,0:T(8,128)(2,1)} %all-gather.11.cloned.1.call-done, bf16[1024,7168]{1,0:T(8,128)(2,1)} %reduce_sum.12, bf16[1024,7168]{1,0:T(8,128)(2,1)} %all-gather.9.cloned.1.call-done), kind=kLoop, calls=%fused_computation.15 | loop fusion | flops 117440512 | bytes 73400320 | tf_op jit(solution)/shard_map/convert_element_type | solution.py:21
  1586.8 0.0 all-gather.13.cloned.1.call-done
  1586.8 0.0 copy-start.1
  1586.8 25.6 %convolution_convert_fusion = bf16[7168,1024]{0,1:T(8,128)(2,1)} fusion(bf16[1024,7168]{1,0:T(8,128)(2,1)} %get-tuple-element.8, bf16[1024,1024]{1,0:T(8,128)(2,1)} %all-gather.13.cloned.1.call-done), kind=kOutput, calls=%fused_computation.19 | convolution fusion | flops 15039725568 | bytes 31457280 | tf_op jit(solution)/shard_map/dot_general | solution.py:8
  1612.3 0.0 copy-done.1
  1612.3 23.5 %convolution_convert_fusion.1 = bf16[7168,1024]{0,1:T(8,128)(2,1)} fusion(bf16[1024,7168]{1,0:T(8,128)(2,1)} %get-tuple-element.9, bf16[1024,1024]{1,0:T(8,128)(2,1)S(1)} %copy-done.1), kind=kOutput, calls=%fused_computation.20 | convolution fusion | flops 15039725568 | bytes 31457280 | tf_op jit(solution)/shard_map/dot_general | solution.py:8
  1635.9 20.6 %pad_maximum_fusion = bf16[7168,2048]{0,1:T(8,128)(2,1)} fusion(bf16[7168,1024]{0,1:T(8,128)(2,1)} %convolution_convert_fusion, bf16[7168,1024]{0,1:T(8,128)(2,1)} %convolution_convert_fusion.1), kind=kLoop, calls=%fused_computation.16 | loop fusion | flops 58720256 | bytes 58720256 | tf_op jit(solution)/shard_map/concatenate | solution.py:56
  1656.5 0.0 reduce-scatter.6.cloned.1.call-update
  1656.5 0.0 reduce-scatter.4.cloned.1.call-start
  1656.6 19.2 %fusion.16 = f32[1024,1024]{1,0:T(8,128)S(1)} fusion(bf16[1024,7168]{1,0:T(8,128)(2,1)} %get-tuple-element.9, bf16[7168,1024]{1,0:T(8,128)(2,1)} %param.11), kind=kOutput, calls=%fused_computation.25 | convolution fusion | flops 15032385536 | bytes 33554432 | tf_op jit(solution)/shard_map/dot_general | solution.py:41
  1675.8 24.9 %add_convert_fusion = bf16[1024,1024]{1,0:T(8,128)(2,1)} fusion(f32[1024,1024]{1,0:T(8,128)S(1)} %fusion.16, bf16[1024,7168]{1,0:T(8,128)(2,1)} %get-tuple-element.8, bf16[7168,1024]{1,0:T(8,128)(2,1)} %param.12), kind=kOutput, calls=%fused_computation.22 | convolution fusion | flops 15034482688 | bytes 35651584 | tf_op jit(solution)/shard_map/dot_general | solution.py:42
  1700.7 0.0 reduce-scatter.4.cloned.1.call-update
  1700.7 0.0 reduce-scatter.8.cloned.1.call-done
  1700.7 6.7 copy.13
  1707.4 167.2 %reduce-scatter.6.cloned.1.call-done = bf16[1792,2048]{0,1:T(8,128)(2,1)} async-done(((bf16[7168,2048]{0,1:T(8,128)(2,1)}), bf16[1792,2048]{0,1:T(8,128)(2,1)}) %reduce-scatter.6.cloned.1.call-update) | async-done | bytes 7340048 | tf_op jit(solution)/shard_map/reduce_scatter | solution.py:55
  1874.7 9.8 fusion.15
  1884.4 8.4 copy.11
  1892.8 8.4 copy.12
  1901.2 8.2 reduce-scatter.4.cloned.1.call-done
Async XLA Ops:
  7.2 38.2 %all-gather.7.cloned.1.call-start = ((), (), s32[]{:S(2)}) async-start(), calls=%async_computation.3 | async-start | bytes 3145728 | tf_op jit(solution)/shard_map/all_gather | solution.py:28
  7.9 291.5 %all-gather.11.cloned.1.call-start = ((), (), s32[]{:S(2)}) async-start(), calls=%async_computation.5 | async-start | bytes 18350080 | tf_op jit(solution)/shard_map/all_gather | solution.py:35
  8.6 543.0 %all-gather.9.cloned.1.call-start = ((), (), s32[]{:S(2)}) async-start(), calls=%async_computation.4 | async-start | bytes 18350080 | tf_op jit(solution)/shard_map/all_gather | solution.py:36
  9.4 1516.4 %all-gather.15.cloned.1.call-start = ((), (), s32[]{:S(2)}) async-start(), calls=%async_computation.10 | async-start | bytes 73400320 | tf_op jit(solution)/shard_map/all_gather | solution.py:31
  67.6 484.1 %copy-start = (bf16[1024,1024]{1,0:T(8,128)(2,1)S(1)}, bf16[1024,1024]{1,0:T(8,128)(2,1)}, u32[]{:S(2)}) copy-start(bf16[1024,1024]{1,0:T(8,128)(2,1)} %all-gather.7.cloned.1.call-done) | copy-start | bytes 6291460
  67.7 1519.1 %all-gather.13.cloned.1.call-start = ((), (), s32[]{:S(2)}) async-start(), calls=%async_computation.7 | async-start | bytes 3145728 | tf_op jit(solution)/shard_map/all_gather | solution.py:27
  68.3 1632.5 %reduce-scatter.8.cloned.1.call-start = ((), (), s32[]{:S(2)}) async-start(), calls=%async_computation.9 | async-start | bytes 18350080 | tf_op jit(solution)/shard_map/reduce_scatter | solution.py:48
  581.1 1293.6 %reduce-scatter.6.cloned.1.call-start = ((), (), s32[]{:S(2)}) async-start(), calls=%async_computation.8 | async-start | bytes 36700160 | tf_op jit(solution)/shard_map/reduce_scatter | solution.py:55
  1586.8 25.6 %copy-start.1 = (bf16[1024,1024]{1,0:T(8,128)(2,1)S(1)}, bf16[1024,1024]{1,0:T(8,128)(2,1)}, u32[]{:S(2)}) copy-start(bf16[1024,1024]{1,0:T(8,128)(2,1)} %all-gather.13.cloned.1.call-done) | copy-start | bytes 6291460
  1656.5 252.9 %reduce-scatter.4.cloned.1.call-start = ((), (), s32[]{:S(2)}) async-start(), calls=%async_computation.6 | async-start | bytes 3145728 | tf_op jit(solution)/shard_map/reduce_scatter | solution.py:39
Sparse Core Ops, SparseCore 0:
  9.5 35.8 all-gather.6
  46.9 252.4 all-gather.10
  301.0 250.6 all-gather.8
  553.1 972.5 all-gather.14
  1527.1 31.2 all-gather.12
  1560.9 110.0 reduce-scatter.7
  1673.6 201.0 reduce-scatter.5
  1877.5 31.8 reduce-scatter.3
